TPU v7x, 32 devices: a whole 2x2x4 slice. The times are simulated.
32 devices in a mesh: dp: 4 (over z), freq: 2 (over core), tm: 4 (over y, x).
Axes of the slice: x: 2, y: 2, z: 4, core: 2. Of those that a mesh axis runs over, the one named last changes fastest.
Arguments:
- patches: bfloat16 [1312, 32, 768], P(('freq', 'tm'), 'dp'), may hold values from -6 to 6
- col_counts: int32 [4], replicated, may hold values from 26 to 27, as said below
- norm_gain: bfloat16 [2, 768], replicated, may hold values from 0.099609375 to 1.8984375
- norm_shift: bfloat16 [2, 768], replicated, may hold values from -3 to 3
- joint_proj: bfloat16 [768, 2304], replicated, may hold values from -0.3125 to 0.3125
- proj_bias: bfloat16 [2, 768], replicated, may hold values from -3 to 3
- out_proj: bfloat16 [768, 768], replicated, may hold values from -0.875 to 0.875
- up_proj: bfloat16 [768, 3072], replicated, may hold values from -0.21875 to 0.21875
- up_bias: bfloat16 [3072], replicated, may hold values from -3 to 3
- down_proj: bfloat16 [3072, 768], replicated, may hold values from -0.109375 to 0.109375
- out_bias: bfloat16 [2, 768], replicated, may hold values from -3 to 3
- cotangent: bfloat16 [1312, 32, 768], P(('freq', 'tm'), 'dp'), may hold values from -6 to 6
Outputs:
- output: bfloat16 [1312, 32, 768], P(('freq', 'tm'), 'dp')
- grad_patches: bfloat16 [1312, 32, 768], P(('freq', 'tm'), 'dp')
- grad_norm_gain: float32 [2, 768], P(None, ('freq', 'tm'))
- grad_norm_shift: float32 [2, 768], P(None, ('freq', 'tm'))
- grad_joint_proj: float32 [768, 2304], P(('freq', 'tm'))
- grad_proj_bias: float32 [2, 768], P(None, ('freq', 'tm'))
- grad_out_proj: float32 [768, 768], P(('freq', 'tm'))
- grad_up_proj: float32 [768, 3072], P(('freq', 'tm'))
- grad_up_bias: float32 [3072], P(('freq', 'tm'))
- grad_down_proj: float32 [3072, 768], P(('freq', 'tm'))
- grad_out_bias: float32 [2, 768], P(None, ('freq', 'tm'))
Inputs may be any that keep to these rules, and one draw needn't show every extreme that they name: `col_counts`: each entry is 26 or 27, and both occur in every draw.
All inputs are finite; a program needn't handle non-finite values.
Results may differ from a plain program's by a relative error of at most 0.019.
Values may be sent and summed in bfloat16 or wider, within the bound.
No kernel may reach another device: no remote copies, remote signals or barrier semaphores. Data moves between devices by JAX's collectives and lax.ppermute only.
A program may use at most 448 MiB of HBM per device.

v0:
```python
import math
import jax
import jax.numpy as jnp
from jax import lax
from jax.sharding import PartitionSpec as P

HEADS = 12
DH = 64
FREQ_ROWS = 12
EPS = 1e-06
NEG = -1000000000.0


def live_slots(col_counts, slot_ids, freq_ids, time_ids, freq_rows, cap_cols):
    table = jnp.arange(col_counts.shape[0], dtype=jnp.int32)
    live_cols = jnp.sum(
        jnp.where(time_ids[:, None] == table[None, :], col_counts[None, :], 0), axis=1
    )
    in_grid = slot_ids < freq_rows * cap_cols
    column_live = slot_ids // freq_rows < live_cols
    extra_live = (time_ids == 0) & (freq_ids == 0)
    return jnp.where(in_grid, column_live, extra_live)


def norm_rows(values, gain, shift):
    centered = values - jnp.mean(values, axis=-1, keepdims=True)
    inverse = lax.rsqrt(jnp.mean(centered * centered, axis=-1, keepdims=True) + EPS)
    return centered * inverse * gain + shift


def gelu_exact(values):
    return jax.nn.gelu(values, approximate=False)


def matmul(left, right):
    return jnp.dot(left, right, preferred_element_type=jnp.float32)


def matmul_tn(left, right):
    return lax.dot_general(
        left, right, (((0,), (0,)), ((), ())), preferred_element_type=jnp.float32
    )


def matmul_nt(left, right):
    return lax.dot_general(
        left, right, (((1,), (1,)), ((), ())), preferred_element_type=jnp.float32
    )


def head_pair(array, offset, lane_width, head_size):
    section = lax.dynamic_slice_in_dim(array, offset, lane_width, 2)
    return section.reshape(section.shape[0], section.shape[1], 2, head_size)


def add_lanes(target, addend, offset):
    current = lax.dynamic_slice_in_dim(target, offset, addend.shape[2], 2)
    return lax.dynamic_update_slice_in_dim(target, current + addend, offset, 2)


def pair_probs(query_pair, key_pair, log_pair, mask, scale):
    scores = (
        jnp.einsum("qchd,kchd->chqk", query_pair, key_pair, preferred_element_type=jnp.float32)
        * scale
        + mask
    )
    return jnp.exp(scores - jnp.transpose(log_pair, (1, 2, 0))[..., None])


def per_device(
    patches,
    col_counts,
    norm_gain,
    norm_shift,
    joint_proj,
    proj_bias,
    out_proj,
    up_proj,
    up_bias,
    down_proj,
    out_bias,
    cotangent,
):
    slots, clips, width = patches.shape
    row_count = slots * clips
    lane_width = 2 * DH
    pair_count = HEADS // 2
    scale = 1.0 / math.sqrt(DH)
    freq_size = lax.axis_size("freq")
    time_size = lax.axis_size("tm")
    freq_rows = FREQ_ROWS // freq_size
    cap_cols = (slots - 2) // freq_rows
    key_count = slots * freq_size * time_size
    slot_ids = jnp.arange(slots, dtype=jnp.int32)
    own_live = live_slots(
        col_counts,
        slot_ids,
        jnp.full((slots,), lax.axis_index("freq"), jnp.int32),
        jnp.full((slots,), lax.axis_index("tm"), jnp.int32),
        freq_rows,
        cap_cols,
    )
    key_ids = jnp.arange(key_count, dtype=jnp.int32)
    key_group = key_ids // slots
    key_live = live_slots(
        col_counts,
        key_ids % slots,
        key_group // time_size,
        key_group % time_size,
        freq_rows,
        cap_cols,
    )
    key_mask = jnp.where(key_live, 0.0, NEG).astype(jnp.float32)
    row_live = (
        jnp.broadcast_to(own_live[:, None], (slots, clips))
        .reshape(row_count, 1)
        .astype(jnp.float32)
    )
    gain_full = norm_gain.astype(jnp.float32)
    shift_full = norm_shift.astype(jnp.float32)
    bias_full = proj_bias.astype(jnp.float32)
    outb_full = out_bias.astype(jnp.float32)
    upb_full = up_bias.astype(jnp.float32)
    inputs = patches.reshape(row_count, width).astype(jnp.float32)
    normed1, ln1_back = jax.vjp(norm_rows, inputs, gain_full[0], shift_full[0])
    normed1_low = normed1.astype(jnp.bfloat16)
    joint = matmul(normed1_low, joint_proj)
    query_low = (joint[:, :width] + bias_full[0]).astype(jnp.bfloat16)
    keys_low = joint[:, width : 2 * width].astype(jnp.bfloat16)
    memory_low = (joint[:, 2 * width :] + bias_full[1]).astype(jnp.bfloat16)
    query3 = query_low.reshape(slots, clips, width)
    key_value = jnp.concatenate([keys_low, memory_low], axis=1).reshape(slots, clips, 2 * width)
    all_memory = lax.all_gather(key_value, ("freq", "tm"), axis=0, tiled=True)

    def forward_pair(number, state):
        mixed_acc, log_acc = state
        offset = number * lane_width
        query_pair = head_pair(query3, offset, lane_width, DH)
        key_pair = head_pair(all_memory, offset, lane_width, DH)
        value_pair = head_pair(all_memory, width + offset, lane_width, DH)
        scores = (
            jnp.einsum("qchd,kchd->chqk", query_pair, key_pair, preferred_element_type=jnp.float32)
            * scale
            + key_mask
        )
        highest = jnp.max(scores, axis=-1, keepdims=True)
        exponent = jnp.exp(scores - highest)
        summed = jnp.sum(exponent, axis=-1, keepdims=True)
        attention = (exponent / summed).astype(jnp.bfloat16)
        mixed = jnp.einsum(
            "chqk,kchd->qchd", attention, value_pair, preferred_element_type=jnp.float32
        )
        log_pair = jnp.transpose((highest + jnp.log(summed))[..., 0], (2, 0, 1))
        mixed_acc = lax.dynamic_update_slice_in_dim(
            mixed_acc, mixed.reshape(slots, clips, lane_width), offset, 2
        )
        log_acc = lax.dynamic_update_slice_in_dim(log_acc, log_pair, 2 * number, 2)
        return (mixed_acc, log_acc)

    mixed_full, log_rows = lax.fori_loop(
        0,
        pair_count,
        forward_pair,
        (
            jnp.zeros((slots, clips, width), jnp.float32),
            jnp.zeros((slots, clips, HEADS), jnp.float32),
        ),
    )
    mixed_low = mixed_full.reshape(row_count, width).astype(jnp.bfloat16)
    middle = inputs + matmul(mixed_low, out_proj) + outb_full[0]
    normed2, ln2_back = jax.vjp(norm_rows, middle, gain_full[1], shift_full[1])
    normed2_low = normed2.astype(jnp.bfloat16)
    pre_act = matmul(normed2_low, up_proj) + upb_full
    activated, gelu_back = jax.vjp(gelu_exact, pre_act)
    hidden_low = activated.astype(jnp.bfloat16)
    final = middle + matmul(hidden_low, down_proj) + outb_full[1]
    output = (final * row_live).astype(jnp.bfloat16).reshape(slots, clips, width)
    grad_out_rows = cotangent.reshape(row_count, width).astype(jnp.float32) * row_live
    grad_out_low = grad_out_rows.astype(jnp.bfloat16)
    grad_down_part = matmul_tn(hidden_low, grad_out_low)
    grad_outb_mlp = jnp.sum(grad_out_rows, axis=0)
    grad_hidden = matmul_nt(grad_out_low, down_proj)
    grad_pre_low = gelu_back(grad_hidden)[0].astype(jnp.bfloat16)
    grad_up_part = matmul_tn(normed2_low, grad_pre_low)
    grad_upb_part = jnp.sum(grad_pre_low.astype(jnp.float32), axis=0)
    grad_normed2 = matmul_nt(grad_pre_low, up_proj)
    grad_mid_part, grad_gain_mlp, grad_shift_mlp = ln2_back(grad_normed2)
    grad_middle = grad_out_rows + grad_mid_part
    grad_branch = grad_middle.astype(jnp.bfloat16)
    grad_outp_part = matmul_tn(mixed_low, grad_branch)
    grad_outb_attn = jnp.sum(grad_branch.astype(jnp.float32), axis=0)
    grad_mixed_low = matmul_nt(grad_branch, out_proj).astype(jnp.bfloat16)
    grad_mixed3 = grad_mixed_low.reshape(slots, clips, width)

    def query_side(number):
        offset = number * lane_width
        query_pair = head_pair(query3, offset, lane_width, DH)
        grad_pair = head_pair(grad_mixed3, offset, lane_width, DH)
        key_pair = head_pair(all_memory, offset, lane_width, DH)
        value_pair = head_pair(all_memory, width + offset, lane_width, DH)
        log_pair = lax.dynamic_slice_in_dim(log_rows, 2 * number, 2, 2)
        probability = pair_probs(query_pair, key_pair, log_pair, key_mask, scale)
        grad_probs = jnp.einsum(
            "qchd,kchd->chqk", grad_pair, value_pair, preferred_element_type=jnp.float32
        )
        delta = jnp.sum(probability * grad_probs, axis=-1, keepdims=True)
        grad_scores = (probability * (grad_probs - delta)).astype(jnp.bfloat16)
        grad_query = (
            jnp.einsum("chqk,kchd->qchd", grad_scores, key_pair, preferred_element_type=jnp.float32)
            * scale
        )
        return (
            offset,
            query_pair,
            grad_pair,
            probability,
            grad_scores,
            delta,
            grad_query.reshape(slots, clips, lane_width),
        )

    zero_query = jnp.zeros((slots, clips, width), jnp.float32)

    def backward_pair(number, state):
        grad_query_acc, grad_memory = state
        side = query_side(number)
        offset = side[0]
        grad_keys = (
            jnp.einsum("chqk,qchd->kchd", side[4], side[1], preferred_element_type=jnp.float32)
            * scale
        )
        grad_values = jnp.einsum(
            "chqk,qchd->kchd",
            side[3].astype(jnp.bfloat16),
            side[2],
            preferred_element_type=jnp.float32,
        )
        grad_memory = add_lanes(
            grad_memory, grad_keys.reshape(key_count, clips, lane_width), offset
        )
        grad_memory = add_lanes(
            grad_memory, grad_values.reshape(key_count, clips, lane_width), width + offset
        )
        return (add_lanes(grad_query_acc, side[6], offset), grad_memory)

    grad_query_full, grad_memory_all = lax.fori_loop(
        0,
        pair_count,
        backward_pair,
        (zero_query, jnp.zeros((key_count, clips, 2 * width), jnp.float32)),
    )
    grad_memory_own = lax.psum_scatter(
        grad_memory_all, ("freq", "tm"), scatter_dimension=0, tiled=True
    )
    grad_query_low = grad_query_full.reshape(row_count, width).astype(jnp.bfloat16)
    grad_memory_low = grad_memory_own.reshape(row_count, 2 * width).astype(jnp.bfloat16)
    grad_joint = jnp.concatenate([grad_query_low, grad_memory_low], axis=1)
    grad_joint_part = matmul_tn(normed1_low, grad_joint)
    grad_bias_cols = jnp.stack(
        [
            jnp.sum(grad_query_low.astype(jnp.float32), axis=0),
            jnp.sum(grad_memory_low[:, width:].astype(jnp.float32), axis=0),
        ],
        axis=1,
    )
    grad_normed1 = matmul_nt(grad_joint, joint_proj)
    grad_in_part, grad_gain_attn, grad_shift_attn = ln1_back(grad_normed1)
    grad_patches = (grad_middle + grad_in_part).astype(jnp.bfloat16).reshape(slots, clips, width)
    shares = (
        lax.psum_scatter(
            grad_joint_part.astype(jnp.bfloat16), ("freq", "tm"), scatter_dimension=0, tiled=True
        ).astype(jnp.float32),
        lax.psum_scatter(
            grad_bias_cols.astype(jnp.bfloat16), ("freq", "tm"), scatter_dimension=0, tiled=True
        ).astype(jnp.float32),
        lax.psum_scatter(
            grad_outp_part.astype(jnp.bfloat16), ("freq", "tm"), scatter_dimension=0, tiled=True
        ).astype(jnp.float32),
        lax.psum_scatter(
            grad_outb_attn.astype(jnp.bfloat16), ("freq", "tm"), scatter_dimension=0, tiled=True
        ).astype(jnp.float32),
        lax.psum_scatter(
            grad_gain_attn.astype(jnp.bfloat16), ("freq", "tm"), scatter_dimension=0, tiled=True
        ).astype(jnp.float32),
        lax.psum_scatter(
            grad_shift_attn.astype(jnp.bfloat16), ("freq", "tm"), scatter_dimension=0, tiled=True
        ).astype(jnp.float32),
        lax.psum_scatter(
            grad_up_part.astype(jnp.bfloat16), ("freq", "tm"), scatter_dimension=0, tiled=True
        ).astype(jnp.float32),
        lax.psum_scatter(
            grad_upb_part.astype(jnp.bfloat16), ("freq", "tm"), scatter_dimension=0, tiled=True
        ).astype(jnp.float32),
        lax.psum_scatter(
            grad_down_part.astype(jnp.bfloat16), ("freq", "tm"), scatter_dimension=0, tiled=True
        ).astype(jnp.float32),
        lax.psum_scatter(
            grad_outb_mlp.astype(jnp.bfloat16), ("freq", "tm"), scatter_dimension=0, tiled=True
        ).astype(jnp.float32),
        lax.psum_scatter(
            grad_gain_mlp.astype(jnp.bfloat16), ("freq", "tm"), scatter_dimension=0, tiled=True
        ).astype(jnp.float32),
        lax.psum_scatter(
            grad_shift_mlp.astype(jnp.bfloat16), ("freq", "tm"), scatter_dimension=0, tiled=True
        ).astype(jnp.float32),
    )
    summed_all = (
        lax.psum(shares[0].astype(jnp.bfloat16), "dp").astype(jnp.float32),
        lax.psum(shares[1].astype(jnp.bfloat16), "dp").astype(jnp.float32),
        lax.psum(shares[2].astype(jnp.bfloat16), "dp").astype(jnp.float32),
        lax.psum(shares[3].astype(jnp.bfloat16), "dp").astype(jnp.float32),
        lax.psum(shares[4].astype(jnp.bfloat16), "dp").astype(jnp.float32),
        lax.psum(shares[5].astype(jnp.bfloat16), "dp").astype(jnp.float32),
        lax.psum(shares[6].astype(jnp.bfloat16), "dp").astype(jnp.float32),
        lax.psum(shares[7].astype(jnp.bfloat16), "dp").astype(jnp.float32),
        lax.psum(shares[8].astype(jnp.bfloat16), "dp").astype(jnp.float32),
        lax.psum(shares[9].astype(jnp.bfloat16), "dp").astype(jnp.float32),
        lax.psum(shares[10].astype(jnp.bfloat16), "dp").astype(jnp.float32),
        lax.psum(shares[11].astype(jnp.bfloat16), "dp").astype(jnp.float32),
    )
    attn_summed = summed_all[:6]
    mlp_summed = summed_all[6:]
    grad_norm_gain = jnp.stack([attn_summed[4], mlp_summed[4]])
    grad_norm_shift = jnp.stack([attn_summed[5], mlp_summed[5]])
    grad_out_bias = jnp.stack([attn_summed[3], mlp_summed[3]])
    grad_proj_bias = jnp.transpose(attn_summed[1])
    return (
        output,
        grad_patches,
        grad_norm_gain,
        grad_norm_shift,
        attn_summed[0],
        grad_proj_bias,
        attn_summed[2],
        mlp_summed[0],
        mlp_summed[1],
        mlp_summed[2],
        grad_out_bias,
    )


def solution(mesh):
    return jax.shard_map(
        per_device,
        mesh=mesh,
        in_specs=(
            P(("freq", "tm"), "dp", None),
            P(),
            P(),
            P(),
            P(),
            P(),
            P(),
            P(),
            P(),
            P(),
            P(),
            P(("freq", "tm"), "dp", None),
        ),
        out_specs=(
            P(("freq", "tm"), "dp", None),
            P(("freq", "tm"), "dp", None),
            P(None, ("freq", "tm")),
            P(None, ("freq", "tm")),
            P(("freq", "tm"), None),
            P(None, ("freq", "tm")),
            P(("freq", "tm"), None),
            P(("freq", "tm"), None),
            P(("freq", "tm")),
            P(("freq", "tm"), None),
            P(None, ("freq", "tm")),
        ),
        check_vma=False,
    )
```

profile of v0, /device:TPU:0, one launch (start us, length us, event | category | flops | bytes accessed | tf_op | source)
XLA Modules:
  0.0 1731.1 jit_solution(16705769092683540999)
XLA Ops:
  18.8 6.9 fusion.65
  36.0 4.9 copy.43
  44.3 144.5 %all-gather.2.cloned.1.call-done = bf16[1312,8,1536]{2,1,0:T(8,128)(2,1)} async-done(((bf16[164,8,1536]{2,1,0:T(8,128)(2,1)}), bf16[1312,8,1536]{2,1,0:T(8,128)(2,1)}) %all-gather.2.cloned.1.call-update) | async-done | bytes 32243728 | tf_op jit(solution)/shard_map/all_gather | solution.py:133
  188.8 42.4 %copy.42 = bf16[1312,8,1536]{0,2,1:T(8,128)(2,1)} copy(bf16[1312,8,1536]{2,1,0:T(8,128)(2,1)} %all-gather.2.cloned.1.call-done) | data formatting | bytes 64487424 | tf_op jit(solution)/shard_map/while | solution.py:160
  231.9 122.6 %while.34 = (s32[]{:T(128)}, bf16[164,8,768]{2,1,0:T(8,128)(2,1)}, f32[164,8,12]{0,2,1:T(8,128)}, bf16[1312,8,1536]{0,2,1:T(8,128)(2,1)}, bf16[164,8,768]{0,2,1:...) while((s32[]{:T(128)}, bf16[164,8,768]{2,1,0:T(8,128)(2,1)}, ...), condition=%wide.region_6.7_spmd, body=%wide.region_3.6_spmd.sunk | while | flops 922637760 | bytes 60295916 | solution.py:160
  242.2 5.1 fusion.126
  262.6 5.1 fusion.126
  283.0 5.1 fusion.126
  303.5 5.1 fusion.126
  323.9 5.1 fusion.126
  344.3 5.1 fusion.126
  354.5 4.6 fusion.74
  360.4 45.8 %multiply_convert_fusion.1 = (bf16[1312,3072]{1,0:T(8,128)(2,1)}, f32[1312,3072]{1,0:T(8,128)}, f32[1312,3072]{1,0:T(8,128)}) fusion(f32[3072]{0:T(1024)S(1)} %copy-done.41, bf16[768,3072]{1,0:T(8,128)(2,1)S(1)} %bitcast.204, f32[1312,768]{1,0:T(8,128)S(1)} %get-tuple-element.504, f32[768]{0:T(1024)S(1)} %copy-done.46, f32[768]{0:T(1024)S(1)} %copy-done.39, ...), kind=kOutput, calls=%fused_computation.34 | convolution fusion | flops 6461841408 | bytes 49082624 | tf_op jit(solution)/shard_map/dot_general | solution.py:36
  406.3 21.5 %fusion.75 = (bf16[3072]{0:T(1024)(128)(2,1)}, bf16[1312,3072]{1,0:T(8,128)(2,1)}) fusion(f32[1312,3072]{1,0:T(8,128)} %get-tuple-element.492, bf16[3072,768]{1,0:T(8,128)(2,1)} %param.25, bf16[164,8,768]{2,1,0:T(8,128)(2,1)} %param.27, f32[1312]{0:T(1024)S(1)} %copy-done.22, f32[1312,3072]{1,0:T(8,128)} %get-tuple-element.505, f32[3072]{0:T(1024)} %convert_element_type.229), kind=kOutput, calls=%fused_computation.178 | convolution fusion | flops 6258299904 | bytes 47062144 | tf_op jit(solution)/shard_map/dot_general | solution.py:46
  427.8 14.1 multiply_reduce_fusion.1
  451.1 21.7 %broadcast_in_dim.96 = f32[1312,8,1536]{0,2,1:T(8,128)} broadcast(f32[]{:T(128)} %constant.301.clone.1), dimensions={} | broadcast | bytes 64487428 | tf_op jit(solution)/shard_map/broadcast_in_dim | solution.py:250
  472.7 478.7 %while.35 = (s32[]{:T(128)}, f32[164,8,768]{2,1,0:T(8,128)}, f32[1312,8,1536]{0,2,1:T(8,128)}, bf16[1312,8,1536]{0,2,1:T(8,128)(2,1)}, bf16[164,8,768]{0,2,1:T(8...) while((s32[]{:T(128)}, f32[164,8,768]{2,1,0:T(8,128)}, ...), condition=%wide.region_14.15_spmd, body=%wide.region_12.14_spmd.sunk | while | flops 2238668288 | bytes 267073456 | solution.py:246
  487.8 7.6 fusion.137
  495.4 11.0 multiply_reduce_fusion.5
  506.5 10.5 multiply_convert_fusion.4
  539.5 7.5 constant_dynamic-update-slice_fusion.10
  547.1 5.7 constant_dynamic-update-slice_fusion.11
  567.5 7.6 fusion.137
  575.2 11.0 multiply_reduce_fusion.5
  586.2 10.5 multiply_convert_fusion.4
  619.3 7.5 constant_dynamic-update-slice_fusion.10
  626.9 5.7 constant_dynamic-update-slice_fusion.11
  647.3 7.6 fusion.137
  655.0 11.0 multiply_reduce_fusion.5
  666.0 10.5 multiply_convert_fusion.4
  699.2 7.5 constant_dynamic-update-slice_fusion.10
  706.6 5.6 constant_dynamic-update-slice_fusion.11
  727.1 7.6 fusion.137
  734.7 11.0 multiply_reduce_fusion.5
  745.8 10.5 multiply_convert_fusion.4
  778.8 7.5 constant_dynamic-update-slice_fusion.10
  786.3 5.6 constant_dynamic-update-slice_fusion.11
  806.8 7.6 fusion.137
  814.4 11.0 multiply_reduce_fusion.5
  825.5 10.5 multiply_convert_fusion.4
  858.5 7.5 constant_dynamic-update-slice_fusion.10
  866.0 5.7 constant_dynamic-update-slice_fusion.11
  886.4 7.6 fusion.137
  894.1 11.0 multiply_reduce_fusion.5
  905.2 10.5 multiply_convert_fusion.4
  938.3 7.5 constant_dynamic-update-slice_fusion.10
  945.8 5.7 constant_dynamic-update-slice_fusion.11
  951.5 67.9 %copy.49 = f32[1312,8,1536]{2,1,0:T(8,128)} copy(f32[1312,8,1536]{0,2,1:T(8,128)} %get-tuple-element.368) | data formatting | bytes 128974848 | tf_op jit(solution)/shard_map/while | solution.py:246
  1019.5 5.2 fusion.41
  1024.8 12.6 convolution_convert_fusion.2
  1038.1 15.0 convolution_convert_fusion.1
  1057.5 334.1 %reduce-scatter.9.cloned.1.call-done = f32[164,8,1536]{2,1,0:T(8,128)} async-done(((f32[1312,8,1536]{2,1,0:T(8,128)}), f32[164,8,1536]{2,1,0:T(8,128)}) %reduce-scatter.9.cloned.1.call-update) | async-done | bytes 8060944 | tf_op jit(solution)/shard_map/reduce_scatter | solution.py:252
  1397.5 8.9 convolution_convert_fusion
  1414.3 11.5 fusion.40
  1428.3 11.0 fusion.69
  1440.2 5.6 fusion.21
  1445.8 27.6 %all-reduce.7 = (bf16[768]{0:T(1024)(128)(2,1)}, bf16[768]{0:T(1024)(128)(2,1)}, bf16[768]{0:T(1024)(128)(2,1)}, bf16[768]{0:T(1024)(128)(2,1)}, bf16[3072]{0:T(...) all-reduce(bf16[768]{0:T(1024)(128)(2,1)} %get-tuple-element.425, ...), channel_id=4, replica_groups=mesh['dp'=4,'freq'=2,'tm'=4] {'freq','tm'}, use_global_device_ids=true, to_apply=%region_22.23.clone | all-reduce | flops 7680 | bytes 30720
  1474.6 15.7 reduce-scatter.17.cloned.1.call-done
  1490.3 57.2 %reduce-scatter.15.cloned.1.call-done = bf16[96,3072]{1,0:T(8,128)(2,1)} async-done(((bf16[768,3072]{1,0:T(8,128)(2,1)}), bf16[96,3072]{1,0:T(8,128)(2,1)}) %reduce-scatter.15.cloned.1.call-update) | async-done | bytes 589840 | tf_op jit(solution)/shard_map/reduce_scatter | solution.py:288
  1547.5 51.8 %reduce-scatter.11.cloned.1.call-done = bf16[96,2304]{1,0:T(8,128)(2,1)} async-done(((bf16[768,2304]{1,0:T(8,128)(2,1)}), bf16[96,2304]{1,0:T(8,128)(2,1)}) %reduce-scatter.11.cloned.1.call-update) | async-done | bytes 442384 | tf_op jit(solution)/shard_map/reduce_scatter | solution.py:270
  1607.7 6.7 fusion.34
  1614.4 22.4 %reduce-scatter.19.cloned.1.call-done = bf16[96,2]{1,0:T(8,128)(2,1)} async-done(((bf16[768,2]{1,0:T(8,128)(2,1)}), bf16[96,2]{1,0:T(8,128)(2,1)}) %reduce-scatter.19.cloned.1.call-update) | async-done | bytes 400
  1637.6 12.7 all-reduce.8
  1655.2 60.9 %all-reduce.12.cloned.1.call-done = (bf16[96,2304]{1,0:T(8,128)(2,1)}, bf16[96,768]{1,0:T(8,128)(2,1)}, bf16[96,3072]{1,0:T(8,128)(2,1)}, bf16[384,768]{1,0:T(8,128)(2,1)}) async-done(((bf16[96,2304]{1,0:T(8,128)(2,1)}, bf16[96,768]{1,0:T(8,128)(2,1)}, bf16[96,3072]{1,0:T(8,128)(2,1)}, bf16[384,768]{1,0:T(8,128)(2,1)}), (bf16[96,2304]{1,0:T(8,128)(2,1)}, bf16[96,768]{1,0:T(8,128)(2,1)}, ...) | async-done | bytes 1769488 | tf_op jit(solution)/shard_map/psum | solution.py:308
  (420 shorter events, 396.5 us)
Async XLA Ops:
  7.2 11.6 copy-start
  7.2 6.0 copy-start.48
  7.2 6.6 copy-start.49
  7.2 181.6 %all-gather.2.cloned.1.call-start = ((), (), s32[]{:S(2)}) async-start(), calls=%async_computation.6 | async-start | bytes 36274176 | tf_op jit(solution)/shard_map/all_gather | solution.py:133
  10.9 14.7 copy-start.20
  17.4 8.3 copy-start.29
  17.4 8.3 copy-start.24
  18.8 6.9 copy-start.33
  18.8 6.9 copy-start.44
  30.7 1360.9 %reduce-scatter.9.cloned.1.call-start = ((), (), s32[]{:S(2)}) async-start(), calls=%async_computation.7 | async-start | bytes 72548352 | tf_op jit(solution)/shard_map/reduce_scatter | solution.py:252
  359.1 47.1 %copy-start.9 = (f32[1312,768]{1,0:T(8,128)}, f32[1312,768]{1,0:T(8,128)S(1)}, u32[]{:S(2)}) copy-start(f32[1312,768]{1,0:T(8,128)S(1)} %get-tuple-element.504) | copy-start | bytes 12091396
  359.2 82.8 %copy-start.31 = (f32[1312]{0:T(1024)}, f32[1312]{0:T(1024)S(1)}, u32[]{:S(2)}) copy-start(f32[1312]{0:T(1024)S(1)} %broadcast_multiply_fusion.1) | copy-start | bytes 15748
  359.8 46.5 %copy-start.35 = (f32[1312]{0:T(1024)}, f32[1312]{0:T(1024)S(1)}, u32[]{:S(2)}) copy-start(f32[1312]{0:T(1024)S(1)} %fusion.60) | copy-start | bytes 15748
  360.4 45.9 %copy-start.22 = (f32[1312]{0:T(1024)S(1)}, f32[1312]{0:T(1024)}, u32[]{:S(2)}) copy-start(f32[1312]{0:T(1024)} %convert_element_type.232) | copy-start | bytes 15748
  427.8 14.1 copy-start.28
  427.8 14.2 copy-start.10
  427.8 14.2 copy-start.36
  427.8 14.2 copy-start.40
  451.1 21.7 %copy-start.15 = (f32[1312]{0:T(1024)S(1)}, f32[1312]{0:T(1024)}, u32[]{:S(2)}) copy-start(f32[1312]{0:T(1024)} %get-tuple-element.731) | copy-start | bytes 15748
  487.7 18.7 %copy-start.2 = (bf16[1312,8,128]{0,2,1:T(8,128)(2,1)}, bf16[1312,8,128]{0,2,1:T(8,128)(2,1)S(1)}, u32[]{:S(2)}) copy-start(bf16[1312,8,128]{0,2,1:T(8,128)(2,1)S(1)} %get-tuple-element.610) | copy-start | bytes 8060932 | tf_op jit(solution)/shard_map/while
  487.7 7.7 copy-start.4
  487.7 7.7 copy-start.19
  506.5 14.0 copy-start.1
  537.3 9.7 slice-start
  539.5 7.5 slice-start.1
  567.5 18.7 %copy-start.2 = (bf16[1312,8,128]{0,2,1:T(8,128)(2,1)}, bf16[1312,8,128]{0,2,1:T(8,128)(2,1)S(1)}, u32[]{:S(2)}) copy-start(bf16[1312,8,128]{0,2,1:T(8,128)(2,1)S(1)} %get-tuple-element.610) | copy-start | bytes 8060932 | tf_op jit(solution)/shard_map/while
  567.5 7.7 copy-start.4
  567.5 7.7 copy-start.19
  586.2 14.0 copy-start.1
  617.1 9.8 slice-start
  619.3 7.6 slice-start.1
  647.3 18.7 %copy-start.2 = (bf16[1312,8,128]{0,2,1:T(8,128)(2,1)}, bf16[1312,8,128]{0,2,1:T(8,128)(2,1)S(1)}, u32[]{:S(2)}) copy-start(bf16[1312,8,128]{0,2,1:T(8,128)(2,1)S(1)} %get-tuple-element.610) | copy-start | bytes 8060932 | tf_op jit(solution)/shard_map/while
  647.3 7.7 copy-start.4
  647.3 7.7 copy-start.19
  666.0 14.0 copy-start.1
  696.9 9.7 slice-start
  699.1 7.5 slice-start.1
  727.0 18.7 %copy-start.2 = (bf16[1312,8,128]{0,2,1:T(8,128)(2,1)}, bf16[1312,8,128]{0,2,1:T(8,128)(2,1)S(1)}, u32[]{:S(2)}) copy-start(bf16[1312,8,128]{0,2,1:T(8,128)(2,1)S(1)} %get-tuple-element.610) | copy-start | bytes 8060932 | tf_op jit(solution)/shard_map/while
  727.0 7.7 copy-start.4
  727.1 7.7 copy-start.19
  745.8 14.0 copy-start.1
  776.6 9.7 slice-start
  778.8 7.5 slice-start.1
  806.7 18.7 %copy-start.2 = (bf16[1312,8,128]{0,2,1:T(8,128)(2,1)}, bf16[1312,8,128]{0,2,1:T(8,128)(2,1)S(1)}, u32[]{:S(2)}) copy-start(bf16[1312,8,128]{0,2,1:T(8,128)(2,1)S(1)} %get-tuple-element.610) | copy-start | bytes 8060932 | tf_op jit(solution)/shard_map/while
  806.7 7.7 copy-start.4
  806.7 7.7 copy-start.19
  825.5 14.0 copy-start.1
  856.3 9.7 slice-start
  858.5 7.5 slice-start.1
  886.4 18.7 %copy-start.2 = (bf16[1312,8,128]{0,2,1:T(8,128)(2,1)}, bf16[1312,8,128]{0,2,1:T(8,128)(2,1)S(1)}, u32[]{:S(2)}) copy-start(bf16[1312,8,128]{0,2,1:T(8,128)(2,1)S(1)} %get-tuple-element.610) | copy-start | bytes 8060932 | tf_op jit(solution)/shard_map/while
  886.4 7.7 copy-start.4
  886.4 7.7 copy-start.19
  905.1 14.0 copy-start.1
  936.0 9.8 slice-start
  938.3 7.5 slice-start.1
  1019.4 455.2 %reduce-scatter.13.cloned.1.call-start = ((), (), s32[]{:S(2)}) async-start(), calls=%async_computation.9 | async-start | bytes 1327104 | tf_op jit(solution)/shard_map/reduce_scatter | solution.py:276
  1024.7 465.6 %reduce-scatter.17.cloned.1.call-start = ((), (), s32[]{:S(2)}) async-start(), calls=%async_computation.11 | async-start | bytes 5308416 | tf_op jit(solution)/shard_map/reduce_scatter | solution.py:294
  1037.4 510.0 %reduce-scatter.15.cloned.1.call-start = ((), (), s32[]{:S(2)}) async-start(), calls=%async_computation.10 | async-start | bytes 5308416 | tf_op jit(solution)/shard_map/reduce_scatter | solution.py:288
  1053.1 546.2 %reduce-scatter.11.cloned.1.call-start = ((), (), s32[]{:S(2)}) async-start(), calls=%async_computation.8 | async-start | bytes 3981312 | tf_op jit(solution)/shard_map/reduce_scatter | solution.py:270
  1057.5 340.0 %copy-start.21 = (f32[1312]{0:T(1024)S(1)}, f32[1312]{0:T(1024)}, u32[]{:S(2)}) copy-start(f32[1312]{0:T(1024)} %copy-done.20) | copy-start | bytes 15748
  1406.4 230.3 %reduce-scatter.19.cloned.1.call-start = ((), (), s32[]{:S(2)}) async-start(), calls=%async_computation.12 | async-start | bytes 221184
  1414.3 11.5 copy-start.13
  1428.3 11.0 copy-start.30
  1440.0 276.1 %all-reduce.12.cloned.1.call-start = ((), (), s32[]{:S(2)}) async-start(), calls=%async_computation.13 | async-start | bytes 3538944 | tf_op jit(solution)/shard_map/psum | solution.py:308
  (49 other events, 173.5 us)
Sparse Core Ops, SparseCore 0:
  30.8 157.9 all-gather.1
  1019.5 372.0 reduce-scatter.8
  1395.4 36.7 reduce-scatter.12
  1435.9 54.3 reduce-scatter.16
  1493.6 53.8 reduce-scatter.14
  1551.2 48.0 reduce-scatter.10
  1603.2 33.4 reduce-scatter.18
  1639.4 76.6 all-reduce.11
where the time goes:
time: 1740 us; the launch traced here: 1730 us
  waiting for transfers between devices  687 us (39%)
  matrix products  398 us (23%)
  local copies, waits for them, and re-layouts  349 us (20%)
  other arithmetic  239 us (14%)
  blocking collectives  40.3 us (2%)
    reduce_scatter x1, waiting for transfers between devices, per_device(): lax.psum_scatter(grad_memory_all, ('freq', 'tm'), scatter_dimension=0, ti...  334 us
    all_gather x1, waiting for transfers between devices, per_device(): all_memory = lax.all_gather(key_value, ('freq', 'tm'), axis=0, tiled=True)  144 us
    dynamic_update_slice x12, other arithmetic, add_lanes(): return lax.dynamic_update_slice_in_dim(target, current + addend, offset, 2)  78.9 us
    dynamic_slice x36, local copies, waits for them, and re-layouts, head_pair(): section = lax.dynamic_slice_in_dim(array, offset, lane_width, 2)  78.8 us
    dot_general x4, matrix products, matmul(): return jnp.dot(left, right, preferred_element_type=jnp.float32)  68.8 us
    while x1, local copies, waits for them, and re-layouts, per_device(): lax.fori_loop(0, pair_count, backward_pair, (zero_query, jnp.zeros((key_c...  67.9 us
    dot_general x6, matrix products, pair_probs(): jnp.einsum('qchd,kchd->chqk', query_pair, key_pair, preferred_element_typ...  66.2 us
    convert_element_type x6, other arithmetic, query_side(): grad_scores = (probability * (grad_probs - delta)).astype(jnp.bfloat16)  62.9 us
  transfers between devices with their start and end apart: 8, of which 7 were waited for; matrix products, arithmetic and copies ran while one was open for 7% of the time, Pallas kernels for 0%

commit v1 on v0

--- a/solution.py
+++ b/solution.py
@@ -305,7 +305,7 @@
         ).astype(jnp.float32),
     )
     summed_all = (
-        lax.psum(shares[0].astype(jnp.bfloat16), "dp").astype(jnp.float32),
+        jnp.sum(lax.all_gather(shares[0].astype(jnp.bfloat16), "dp"), axis=0).astype(jnp.float32),
         lax.psum(shares[1].astype(jnp.bfloat16), "dp").astype(jnp.float32),
         lax.psum(shares[2].astype(jnp.bfloat16), "dp").astype(jnp.float32),
         lax.psum(shares[3].astype(jnp.bfloat16), "dp").astype(jnp.float32),

time: 1740 us -> 1650 us (0.948)
  waiting for transfers between devices: 687 us -> 583 us
    reduce_scatter x1, waiting for transfers between devices: 57.2 us -> 0.01 us  [per_device(): lax.psum_scatter(grad_up_part.astype(jnp.bfloat16), ('freq', 'tm'), scatt...]
    reduce_scatter x1, waiting for transfers between devices: 334 us -> 368 us  [per_device(): lax.psum_scatter(grad_memory_all, ('freq', 'tm'), scatter_dimension=0, ti...]
    psum x1, waiting for transfers between devices: 60.9 us -> 29.7 us  [per_device(): lax.psum(shares[2].astype(jnp.bfloat16), 'dp').astype(jnp.float32)]
    unnamed x9 -> x10, waiting for transfers between devices: 22.5 us -> 0.15 us
    reduce_scatter x1, waiting for transfers between devices: 51.8 us -> 29.6 us  [per_device(): lax.psum_scatter(grad_joint_part.astype(jnp.bfloat16), ('freq', 'tm'), sc...]
  transfers between devices with their start and end apart: 8 -> 9, of which waited for: 7 -> 5; matrix products, arithmetic and copies ran while one was open for 7% -> 42% of each run, Pallas kernels for 0% -> 0%
where the time goes in v1:
time: 1650 us; the launch traced here: 1630 us
  waiting for transfers between devices  583 us (35%)
  matrix products  396 us (24%)
  local copies, waits for them, and re-layouts  354 us (21%)
  other arithmetic  243 us (15%)
  blocking collectives  40.1 us (2%)
    reduce_scatter x1, waiting for transfers between devices, per_device(): lax.psum_scatter(grad_memory_all, ('freq', 'tm'), scatter_dimension=0, ti...  368 us
    all_gather x1, waiting for transfers between devices, per_device(): all_memory = lax.all_gather(key_value, ('freq', 'tm'), axis=0, tiled=True)  144 us
    dynamic_update_slice x12, other arithmetic, add_lanes(): return lax.dynamic_update_slice_in_dim(target, current + addend, offset, 2)  79.1 us
    dynamic_slice x36, local copies, waits for them, and re-layouts, head_pair(): section = lax.dynamic_slice_in_dim(array, offset, lane_width, 2)  79.1 us
    dot_general x4, matrix products, matmul(): return jnp.dot(left, right, preferred_element_type=jnp.float32)  68.5 us
    while x1, local copies, waits for them, and re-layouts, per_device(): lax.fori_loop(0, pair_count, backward_pair, (zero_query, jnp.zeros((key_c...  67.7 us
    dot_general x6, matrix products, pair_probs(): jnp.einsum('qchd,kchd->chqk', query_pair, key_pair, preferred_element_typ...  66.2 us
    convert_element_type x6, other arithmetic, query_side(): grad_scores = (probability * (grad_probs - delta)).astype(jnp.bfloat16)  63 us
  transfers between devices with their start and end apart: 9, of which 5 were waited for; matrix products, arithmetic and copies ran while one was open for 42% of the time, Pallas kernels for 0%

profile of v1, /device:TPU:0, one launch (start us, length us, event | category | flops | bytes accessed | tf_op | source)
XLA Modules:
  0.0 1634.8 jit_solution(5558651745290250847)
XLA Ops:
  18.8 6.9 fusion.65
  36.0 4.9 copy.43
  44.4 144.4 %all-gather.4.cloned.1.call-done = bf16[1312,8,1536]{2,1,0:T(8,128)(2,1)} async-done(((bf16[164,8,1536]{2,1,0:T(8,128)(2,1)}), bf16[1312,8,1536]{2,1,0:T(8,128)(2,1)}) %all-gather.4.cloned.1.call-update) | async-done | bytes 32243728 | tf_op jit(solution)/shard_map/all_gather | solution.py:133
  188.8 42.4 %copy.42 = bf16[1312,8,1536]{0,2,1:T(8,128)(2,1)} copy(bf16[1312,8,1536]{2,1,0:T(8,128)(2,1)} %all-gather.4.cloned.1.call-done) | data formatting | bytes 64487424 | tf_op jit(solution)/shard_map/while | solution.py:160
  231.9 122.6 %while.34 = (s32[]{:T(128)}, bf16[164,8,768]{2,1,0:T(8,128)(2,1)}, f32[164,8,12]{0,2,1:T(8,128)}, bf16[1312,8,1536]{0,2,1:T(8,128)(2,1)}, bf16[164,8,768]{0,2,1:...) while((s32[]{:T(128)}, bf16[164,8,768]{2,1,0:T(8,128)(2,1)}, ...), condition=%wide.region_6.7_spmd, body=%wide.region_3.6_spmd.sunk | while | flops 922637760 | bytes 60295916 | solution.py:160
  242.2 5.1 fusion.126
  262.6 5.1 fusion.126
  283.0 5.1 fusion.126
  303.5 5.1 fusion.126
  323.9 5.1 fusion.126
  344.3 5.1 fusion.126
  354.5 4.6 fusion.74
  360.9 45.8 %multiply_convert_fusion.1 = (bf16[1312,3072]{1,0:T(8,128)(2,1)}, f32[1312,3072]{1,0:T(8,128)}, f32[1312,3072]{1,0:T(8,128)}) fusion(f32[3072]{0:T(1024)S(1)} %copy-done.42, bf16[768,3072]{1,0:T(8,128)(2,1)S(1)} %bitcast.206, f32[1312,768]{1,0:T(8,128)S(1)} %get-tuple-element.503, f32[768]{0:T(1024)S(1)} %copy-done.49, f32[768]{0:T(1024)S(1)} %copy-done.39, ...), kind=kOutput, calls=%fused_computation.34 | convolution fusion | flops 6461841408 | bytes 49082624 | tf_op jit(solution)/shard_map/dot_general | solution.py:36
  406.7 21.5 %fusion.75 = (bf16[3072]{0:T(1024)(128)(2,1)}, bf16[1312,3072]{1,0:T(8,128)(2,1)}) fusion(f32[1312,3072]{1,0:T(8,128)} %get-tuple-element.491, bf16[3072,768]{1,0:T(8,128)(2,1)} %param.25, bf16[164,8,768]{2,1,0:T(8,128)(2,1)} %param.27, f32[1312]{0:T(1024)S(1)} %copy-done.23, f32[1312,3072]{1,0:T(8,128)} %get-tuple-element.504, f32[3072]{0:T(1024)} %convert_element_type.231), kind=kOutput, calls=%fused_computation.178 | convolution fusion | flops 6258299904 | bytes 47062144 | tf_op jit(solution)/shard_map/dot_general | solution.py:46
  428.2 14.1 multiply_reduce_fusion.1
  450.4 12.5 convolution_convert_fusion.2
  463.0 5.1 fusion.39
  468.1 13.2 convolution_convert_fusion.1
  483.6 23.7 %broadcast_in_dim.96 = f32[1312,8,1536]{0,2,1:T(8,128)} broadcast(f32[]{:T(128)} %constant.302.clone.1), dimensions={} | broadcast | bytes 64487428 | tf_op jit(solution)/shard_map/broadcast_in_dim | solution.py:250
  507.3 480.6 %while.35 = (s32[]{:T(128)}, f32[164,8,768]{2,1,0:T(8,128)}, f32[1312,8,1536]{0,2,1:T(8,128)}, bf16[1312,8,1536]{0,2,1:T(8,128)(2,1)}, bf16[164,8,768]{0,2,1:T(8...) while((s32[]{:T(128)}, f32[164,8,768]{2,1,0:T(8,128)}, ...), condition=%wide.region_14.15_spmd, body=%wide.region_12.14_spmd.sunk | while | flops 2238668288 | bytes 267073456 | solution.py:246
  522.7 7.6 fusion.137
  530.4 11.0 multiply_reduce_fusion.5
  541.4 10.6 multiply_convert_fusion.4
  560.6 4.8 convolution_multiply_fusion.4
  575.7 7.6 constant_dynamic-update-slice_fusion.10
  583.4 5.8 constant_dynamic-update-slice_fusion.11
  604.0 7.6 fusion.137
  611.7 11.0 multiply_reduce_fusion.5
  622.7 10.5 multiply_convert_fusion.4
  641.1 4.6 convolution_multiply_fusion.4
  655.8 7.5 constant_dynamic-update-slice_fusion.10
  663.4 5.7 constant_dynamic-update-slice_fusion.11
  683.9 7.6 fusion.137
  691.5 11.0 multiply_reduce_fusion.5
  702.6 10.5 multiply_convert_fusion.4
  735.6 7.5 constant_dynamic-update-slice_fusion.10
  743.1 5.6 constant_dynamic-update-slice_fusion.11
  763.5 7.6 fusion.137
  771.2 11.0 multiply_reduce_fusion.5
  782.3 10.5 multiply_convert_fusion.4
  815.3 7.5 constant_dynamic-update-slice_fusion.10
  822.8 5.6 constant_dynamic-update-slice_fusion.11
  843.2 7.6 fusion.137
  850.8 11.0 multiply_reduce_fusion.5
  861.9 10.5 multiply_convert_fusion.4
  895.0 7.5 constant_dynamic-update-slice_fusion.10
  902.5 5.7 constant_dynamic-update-slice_fusion.11
  922.9 7.6 fusion.137
  930.6 11.0 multiply_reduce_fusion.5
  941.6 10.5 multiply_convert_fusion.4
  974.8 7.5 constant_dynamic-update-slice_fusion.10
  982.3 5.7 constant_dynamic-update-slice_fusion.11
  987.9 67.7 %copy.49 = f32[1312,8,1536]{2,1,0:T(8,128)} copy(f32[1312,8,1536]{0,2,1:T(8,128)} %get-tuple-element.368) | data formatting | bytes 128974848 | tf_op jit(solution)/shard_map/while | solution.py:246
  1059.4 368.3 %reduce-scatter.9.cloned.1.call-done = f32[164,8,1536]{2,1,0:T(8,128)} async-done(((f32[1312,8,1536]{2,1,0:T(8,128)}), f32[164,8,1536]{2,1,0:T(8,128)}) %reduce-scatter.9.cloned.1.call-update) | async-done | bytes 8060944 | tf_op jit(solution)/shard_map/reduce_scatter | solution.py:252
  1433.7 8.8 convolution_convert_fusion
  1451.1 11.2 fusion.40
  1462.3 29.7 %all-reduce.12.cloned.1.call-done = (bf16[96,768]{1,0:T(8,128)(2,1)}, bf16[96,3072]{1,0:T(8,128)(2,1)}, bf16[384,768]{1,0:T(8,128)(2,1)}) async-done(((bf16[96,768]{1,0:T(8,128)(2,1)}, bf16[96,3072]{1,0:T(8,128)(2,1)}, bf16[384,768]{1,0:T(8,128)(2,1)}), (bf16[96,768]{1,0:T(8,128)(2,1)}, bf16[96,3072]{1,0:T(8,128)(2,1)}, bf16[384,768]{1,0:T(8,128)(2,1)})) %all-reduce.12.cloned.1.call-update) | async-done | bytes 1327120 | tf_op jit(solution)/shard_map/psum | solution.py:310
  1502.3 11.7 fusion.69
  1514.0 29.6 %reduce-scatter.11.cloned.1.call-done = bf16[96,2304]{1,0:T(8,128)(2,1)} async-done(((bf16[768,2304]{1,0:T(8,128)(2,1)}), bf16[96,2304]{1,0:T(8,128)(2,1)}) %reduce-scatter.11.cloned.1.call-update) | async-done | bytes 442384 | tf_op jit(solution)/shard_map/reduce_scatter | solution.py:270
  1544.9 5.1 fusion.21
  1550.0 27.0 %all-reduce.7 = (bf16[768]{0:T(1024)(128)(2,1)}, bf16[768]{0:T(1024)(128)(2,1)}, bf16[768]{0:T(1024)(128)(2,1)}, bf16[768]{0:T(1024)(128)(2,1)}, bf16[3072]{0:T(...) all-reduce(bf16[768]{0:T(1024)(128)(2,1)} %get-tuple-element.425, ...), channel_id=5, replica_groups=mesh['dp'=4,'freq'=2,'tm'=4] {'freq','tm'}, use_global_device_ids=true, to_apply=%region_22.23.clone | all-reduce | flops 7680 | bytes 30720
  1586.6 6.9 fusion.34
  1594.4 13.1 all-reduce.8
  1612.3 11.2 all-gather.6.cloned.1.call-done
  (428 shorter events, 394.2 us)
Async XLA Ops:
  7.2 11.6 copy-start
  7.2 6.6 copy-start.52
  7.2 181.6 %all-gather.4.cloned.1.call-start = ((), (), s32[]{:S(2)}) async-start(), calls=%async_computation.6 | async-start | bytes 36274176 | tf_op jit(solution)/shard_map/all_gather | solution.py:133
  10.9 14.7 copy-start.21
  17.4 8.3 copy-start.31
  17.4 8.3 copy-start.26
  18.8 6.9 copy-start.32
  18.8 6.9 copy-start.46
  30.7 1028.6 %reduce-scatter.13.cloned.1.call-start = ((), (), s32[]{:S(2)}) async-start(), calls=%async_computation.9 | async-start | bytes 1327104 | tf_op jit(solution)/shard_map/reduce_scatter | solution.py:276
  359.1 47.6 %copy-start.9 = (f32[1312,768]{1,0:T(8,128)}, f32[1312,768]{1,0:T(8,128)S(1)}, u32[]{:S(2)}) copy-start(f32[1312,768]{1,0:T(8,128)S(1)} %get-tuple-element.503) | copy-start | bytes 12091396
  359.8 46.9 %copy-start.34 = (f32[1312]{0:T(1024)}, f32[1312]{0:T(1024)S(1)}, u32[]{:S(2)}) copy-start(f32[1312]{0:T(1024)S(1)} %fusion.60) | copy-start | bytes 15748
  360.8 45.9 %copy-start.23 = (f32[1312]{0:T(1024)S(1)}, f32[1312]{0:T(1024)}, u32[]{:S(2)}) copy-start(f32[1312]{0:T(1024)} %convert_element_type.234) | copy-start | bytes 15748
  428.2 14.1 copy-start.30
  428.2 14.1 copy-start.10
  428.2 14.2 copy-start.35
  428.2 14.2 copy-start.40
  450.4 608.9 %reduce-scatter.17.cloned.1.call-start = ((), (), s32[]{:S(2)}) async-start(), calls=%async_computation.11 | async-start | bytes 5308416 | tf_op jit(solution)/shard_map/reduce_scatter | solution.py:294
  462.9 596.4 %reduce-scatter.15.cloned.1.call-start = ((), (), s32[]{:S(2)}) async-start(), calls=%async_computation.10 | async-start | bytes 5308416 | tf_op jit(solution)/shard_map/reduce_scatter | solution.py:288
  481.3 946.4 %reduce-scatter.9.cloned.1.call-start = ((), (), s32[]{:S(2)}) async-start(), calls=%async_computation.7 | async-start | bytes 72548352 | tf_op jit(solution)/shard_map/reduce_scatter | solution.py:252
  483.6 23.7 %copy-start.15 = (f32[1312]{0:T(1024)S(1)}, f32[1312]{0:T(1024)}, u32[]{:S(2)}) copy-start(f32[1312]{0:T(1024)} %get-tuple-element.729) | copy-start | bytes 15748
  522.7 18.7 %copy-start.2 = (bf16[1312,8,128]{0,2,1:T(8,128)(2,1)}, bf16[1312,8,128]{0,2,1:T(8,128)(2,1)S(1)}, u32[]{:S(2)}) copy-start(bf16[1312,8,128]{0,2,1:T(8,128)(2,1)S(1)} %get-tuple-element.609) | copy-start | bytes 8060932 | tf_op jit(solution)/shard_map/while
  522.7 7.7 copy-start.4
  522.7 7.7 copy-start.20
  541.4 14.6 copy-start.1
  573.5 9.9 slice-start
  575.7 7.6 slice-start.1
  604.0 18.7 %copy-start.2 = (bf16[1312,8,128]{0,2,1:T(8,128)(2,1)}, bf16[1312,8,128]{0,2,1:T(8,128)(2,1)S(1)}, u32[]{:S(2)}) copy-start(bf16[1312,8,128]{0,2,1:T(8,128)(2,1)S(1)} %get-tuple-element.609) | copy-start | bytes 8060932 | tf_op jit(solution)/shard_map/while
  604.0 7.7 copy-start.4
  604.0 7.7 copy-start.20
  622.7 14.0 copy-start.1
  653.6 9.8 slice-start
  655.8 7.6 slice-start.1
  683.8 18.7 %copy-start.2 = (bf16[1312,8,128]{0,2,1:T(8,128)(2,1)}, bf16[1312,8,128]{0,2,1:T(8,128)(2,1)S(1)}, u32[]{:S(2)}) copy-start(bf16[1312,8,128]{0,2,1:T(8,128)(2,1)S(1)} %get-tuple-element.609) | copy-start | bytes 8060932 | tf_op jit(solution)/shard_map/while
  683.9 7.7 copy-start.4
  683.9 7.7 copy-start.20
  702.6 14.0 copy-start.1
  733.5 9.7 slice-start
  735.6 7.5 slice-start.1
  763.5 18.7 %copy-start.2 = (bf16[1312,8,128]{0,2,1:T(8,128)(2,1)}, bf16[1312,8,128]{0,2,1:T(8,128)(2,1)S(1)}, u32[]{:S(2)}) copy-start(bf16[1312,8,128]{0,2,1:T(8,128)(2,1)S(1)} %get-tuple-element.609) | copy-start | bytes 8060932 | tf_op jit(solution)/shard_map/while
  763.5 7.7 copy-start.4
  763.5 7.7 copy-start.20
  782.2 14.0 copy-start.1
  813.1 9.6 slice-start
  815.3 7.5 slice-start.1
  843.1 18.7 %copy-start.2 = (bf16[1312,8,128]{0,2,1:T(8,128)(2,1)}, bf16[1312,8,128]{0,2,1:T(8,128)(2,1)S(1)}, u32[]{:S(2)}) copy-start(bf16[1312,8,128]{0,2,1:T(8,128)(2,1)S(1)} %get-tuple-element.609) | copy-start | bytes 8060932 | tf_op jit(solution)/shard_map/while
  843.2 7.7 copy-start.4
  843.2 7.7 copy-start.20
  861.9 14.0 copy-start.1
  892.8 9.7 slice-start
  895.0 7.5 slice-start.1
  922.9 18.7 %copy-start.2 = (bf16[1312,8,128]{0,2,1:T(8,128)(2,1)}, bf16[1312,8,128]{0,2,1:T(8,128)(2,1)S(1)}, u32[]{:S(2)}) copy-start(bf16[1312,8,128]{0,2,1:T(8,128)(2,1)S(1)} %get-tuple-element.609) | copy-start | bytes 8060932 | tf_op jit(solution)/shard_map/while
  922.9 7.7 copy-start.4
  922.9 7.7 copy-start.20
  941.6 14.0 copy-start.1
  972.5 9.8 slice-start
  974.8 7.5 slice-start.1
  1055.6 436.3 %all-reduce.12.cloned.1.call-start = ((), (), s32[]{:S(2)}) async-start(), calls=%async_computation.14 | async-start | bytes 2654208 | tf_op jit(solution)/shard_map/psum | solution.py:310
  1059.4 374.3 %copy-start.22 = (f32[1312]{0:T(1024)S(1)}, f32[1312]{0:T(1024)}, u32[]{:S(2)}) copy-start(f32[1312]{0:T(1024)} %copy-done.21) | copy-start | bytes 15748
  1059.4 374.3 %copy-start.27 = (f32[1312]{0:T(1024)S(1)}, f32[1312]{0:T(1024)}, u32[]{:S(2)}) copy-start(f32[1312]{0:T(1024)} %copy-done.26) | copy-start | bytes 15748
  1059.4 484.2 %reduce-scatter.11.cloned.1.call-start = ((), (), s32[]{:S(2)}) async-start(), calls=%async_computation.8 | async-start | bytes 3981312 | tf_op jit(solution)/shard_map/reduce_scatter | solution.py:270
  1442.6 8.5 copy-start.24
  1442.6 151.0 %reduce-scatter.19.cloned.1.call-start = ((), (), s32[]{:S(2)}) async-start(), calls=%async_computation.13 | async-start | bytes 221184
  1491.9 7.9 copy-start.43
  1502.0 121.5 %all-gather.6.cloned.1.call-start = ((), (), s32[]{:S(2)}) async-start(), calls=%async_computation.12 | async-start | bytes 2211840 | tf_op jit(solution)/shard_map/all_gather | solution.py:308
  (52 other events, 192.4 us)
Sparse Core Ops, SparseCore 0:
  30.8 157.9 all-gather.3
  450.5 36.7 reduce-scatter.12
  491.1 53.8 reduce-scatter.16
  548.4 53.8 reduce-scatter.14
  1055.8 371.9 reduce-scatter.8
  1430.3 61.5 all-reduce.11
  1495.8 47.7 reduce-scatter.10
  1547.5 33.4 reduce-scatter.18
  1582.6 40.8 all-gather.5
